TPU v7x, 32 devices: a whole 2x2x4 slice. The times are simulated.
32 devices in a mesh: face: 2 (over y), ty: 4 (over x, core), tx: 4 (over z).
Axes of the slice: x: 2, y: 2, z: 4, core: 2. Of those that a mesh axis runs over, the one named last changes fastest.
Arguments:
- cotangent: float32 [2, 32, 32, 128], P('face', 'ty', 'tx'), may hold values from -6 to 6
- courant_x: float32 [2, 32, 36, 32], P('face', 'ty', 'tx'), may hold values from -0.6 to 0.6
- edge_x: float32 [2, 32, 36], P('face', 'ty', 'tx'), may hold values from 0.7 to 1.4
- courant_y: float32 [2, 36, 32, 32], P('face', 'ty', 'tx'), may hold values from -0.6 to 0.6
- edge_y: float32 [2, 36, 32], P('face', 'ty', 'tx'), may hold values from 0.7 to 1.4
- cell_area: float32 [2, 32, 32], P('face', 'ty', 'tx'), may hold values from 0.7 to 1.4
- seam_partner: int32 [2, 4], replicated, may hold values from 0 to 7, as said below
- seam_flip: int32 [2, 4], replicated, may hold values from 0 to 1, as said below
Outputs:
- sensitivity: float32 [2, 32, 32, 128], P('face', 'ty', 'tx')
Inputs may be any that keep to these rules, and one draw needn't show every extreme that they name: `seam_partner`: the gluing pairs face edges: the partner of an edge's partner is that edge, and no edge is glued to itself; some east or west edge is glued to a north or south edge. `seam_flip`: the same for both edges of a glued pair.
All inputs are finite; a program needn't handle non-finite values.
Results may differ from a plain program's by a relative error of at most 0.0003.
Values sent between devices are 32-bit elements; how exact they have to be, the bound alone decides.
No kernel may reach another device: no remote copies, remote signals or barrier semaphores. Data moves between devices by JAX's collectives and lax.ppermute only.
A program may use at most 64 MiB of HBM per device.

v0:
```python
import jax
import jax.numpy as jnp
from jax import lax
from jax.sharding import PartitionSpec as P

STEPS = 2


def padded(cells, sides, width):
    for axis, dim in sides:
        count = lax.axis_size(axis)
        ends = count - 1
        head = lax.slice_in_dim(cells, 0, width, axis=dim)
        tail = lax.slice_in_dim(cells, cells.shape[dim] - width, cells.shape[dim], axis=dim)
        cells = jnp.concatenate(
            [
                lax.ppermute(tail, axis, [(i, (i + 1) % count) for i in range(ends)]),
                cells,
                lax.ppermute(head, axis, [((i + 1) % count, i) for i in range(ends)]),
            ],
            axis=dim,
        )
    return cells


def take_slab(source, axis_at, anchor, finish):
    return lax.slice_in_dim(source, anchor, finish, axis=axis_at)


def parabolic_sweep(extended, courant, edge_length, area_cells, axis_at):
    inner_count = extended.shape[axis_at] - 6
    interface_value = 7.0 / 12.0 * (
        take_slab(extended, axis_at, 1, inner_count + 4)
        + take_slab(extended, axis_at, 2, inner_count + 5)
    ) - 1.0 / 12.0 * (
        take_slab(extended, axis_at, 0, inner_count + 3)
        + take_slab(extended, axis_at, 3, inner_count + 6)
    )
    a_low = take_slab(interface_value, axis_at, 0, inner_count + 1)
    a_mid = take_slab(interface_value, axis_at, 1, inner_count + 2)
    a_high = take_slab(interface_value, axis_at, 2, inner_count + 3)
    left_cell = take_slab(extended, axis_at, 2, inner_count + 3)
    right_cell = take_slab(extended, axis_at, 3, inner_count + 4)
    curve_left = 6.0 * left_cell - 3.0 * (a_low + a_mid)
    curve_right = 6.0 * right_cell - 3.0 * (a_mid + a_high)
    upwind = -courant
    from_left = a_mid - 0.5 * courant * (a_mid - a_low - (1.0 - courant * (2.0 / 3.0)) * curve_left)
    from_right = a_mid + 0.5 * upwind * (
        a_high - a_mid + (1.0 - upwind * (2.0 / 3.0)) * curve_right
    )
    face_value = jnp.where(courant > 0, from_left, from_right)
    flux_term = courant * edge_length * face_value
    return (
        take_slab(extended, axis_at, 3, inner_count + 3)
        - (
            take_slab(flux_term, axis_at, 1, inner_count + 1)
            - take_slab(flux_term, axis_at, 0, inner_count)
        )
        / area_cells
    )


def indicator(flag):
    return flag.astype(jnp.float32)


def on_device(cotangent, courant_x, edge_x, courant_y, edge_y, cell_area, seam_partner, seam_flip):
    adjoint = cotangent[0]
    height_cells, width_cells, lanes_all = adjoint.shape
    repeat_count = lanes_all // courant_x.shape[-1]
    tiles_wide = lax.axis_size("tx")
    tiles_high = lax.axis_size("ty")
    face_index = lax.axis_index("face")
    row_index = lax.axis_index("ty")
    column_index = lax.axis_index("tx")
    spread_x = jnp.tile(courant_x[0], repeat_count)
    length_x = edge_x[0][:, :, None]
    spread_y = jnp.tile(courant_y[0], repeat_count)
    length_y = edge_y[0][:, :, None]
    area_cells = cell_area[0][:, :, None]
    own_codes = lax.dynamic_index_in_dim(seam_partner, face_index, 0, keepdims=False)
    own_flips = lax.dynamic_index_in_dim(seam_flip, face_index, 0, keepdims=False)
    on_east = indicator(column_index == tiles_wide - 1)
    on_west = indicator(column_index == 0)
    on_north = indicator(row_index == tiles_high - 1)
    on_south = indicator(row_index == 0)

    def deliver(strips, parity):
        gathered = lax.all_gather(strips[None], "face", axis=0, tiled=True)
        result = jnp.zeros((height_cells, width_cells, lanes_all), jnp.float32)
        for border in range(4):
            code = own_codes[border]
            other_face = code // 4
            other_border = code % 4
            active = indicator(other_border % 2 == parity)
            chosen = lax.dynamic_index_in_dim(gathered, other_face, 0, keepdims=False)
            chosen = lax.dynamic_index_in_dim(chosen, other_border // 2, 0, keepdims=False)
            chosen = jnp.where(own_flips[border] == 1, chosen[:, ::-1], chosen)
            if border == 0 or border == 2:
                segment = lax.dynamic_slice_in_dim(
                    chosen, row_index * height_cells, height_cells, 1
                )
                columns = jnp.swapaxes(segment, 0, 1)
                if border == 0:
                    result = result.at[:, width_cells - 3 :].add(
                        columns[:, ::-1] * (active * on_east)
                    )
                else:
                    result = result.at[:, :3].add(columns * (active * on_west))
            else:
                segment = lax.dynamic_slice_in_dim(
                    chosen, column_index * width_cells, width_cells, 1
                )
                if border == 1:
                    result = result.at[height_cells - 3 :].add(segment[::-1] * (active * on_north))
                else:
                    result = result.at[:3].add(segment * (active * on_south))
        return result

    def reverse_x(current):
        blank = jnp.zeros((height_cells, width_cells + 6, lanes_all), jnp.float32)

        def sweep_x(extended):
            return parabolic_sweep(extended, spread_x, length_x, area_cells, 1)

        unused, pullback = jax.vjp(sweep_x, blank)
        halo_adjoint = pullback(current)[0]
        own_part = halo_adjoint[:, 3 : width_cells + 3]
        west_rim = halo_adjoint[:, :3]
        east_rim = halo_adjoint[:, width_cells + 3 :]
        packed = jnp.concatenate([west_rim, east_rim], axis=1)
        bordered = padded(packed, (("tx", 1),), 3)
        own_part = (
            own_part.at[:, :3].add(bordered[:, :3]).at[:, width_cells - 3 :].add(bordered[:, 9:])
        )
        east_piece = jnp.swapaxes(east_rim, 0, 1) * on_east
        west_piece = jnp.swapaxes(west_rim[:, ::-1], 0, 1) * on_west
        pieces = jnp.stack([east_piece, west_piece])
        row_total = lax.psum(pieces, "tx")
        strips = lax.all_gather(row_total, "ty", axis=2, tiled=True)
        return own_part + deliver(strips, 0)

    def reverse_y(current):
        blank = jnp.zeros((height_cells + 6, width_cells, lanes_all), jnp.float32)

        def sweep_y(extended):
            return parabolic_sweep(extended, spread_y, length_y, area_cells, 0)

        unused, pullback = jax.vjp(sweep_y, blank)
        halo_adjoint = pullback(current)[0]
        own_part = halo_adjoint[3 : height_cells + 3]
        south_rim = halo_adjoint[:3]
        north_rim = halo_adjoint[height_cells + 3 :]
        packed = jnp.concatenate([south_rim, north_rim], axis=0)
        bordered = padded(packed, (("ty", 0),), 3)
        own_part = own_part.at[:3].add(bordered[:3]).at[height_cells - 3 :].add(bordered[9:])
        north_piece = north_rim * on_north
        south_piece = south_rim[::-1] * on_south
        pieces = jnp.stack([north_piece, south_piece])
        column_total = lax.psum(pieces, "ty")
        strips = lax.all_gather(column_total, "tx", axis=2, tiled=True)
        return own_part + deliver(strips, 1)

    for repeat in range(STEPS):
        adjoint = reverse_y(adjoint)
        adjoint = reverse_x(adjoint)
    return adjoint[None]


def solution(mesh):
    placed = (
        P("face", "ty", "tx", None),
        P("face", "ty", "tx", None),
        P("face", "ty", "tx"),
        P("face", "ty", "tx", None),
        P("face", "ty", "tx"),
        P("face", "ty", "tx"),
        P(),
        P(),
    )
    return jax.shard_map(
        on_device,
        mesh=mesh,
        in_specs=placed,
        out_specs=P("face", "ty", "tx", None),
        check_vma=False,
    )
```

profile of v0, /device:TPU:0, one launch (start us, length us, event | category | flops | bytes accessed | tf_op | source)
XLA Modules:
  0.0 164.9 jit_solution(16922162289223766744)
XLA Ops:
  0.0 0.8 copy.66
  0.8 0.8 tile.21
  1.6 0.0 copy-start
  1.6 0.1 tile.22
  1.7 0.6 copy-done
  2.3 0.1 fusion.68
  2.4 0.0 copy-start.2
  2.4 0.7 copy-done.2
  3.1 0.1 fusion.17
  3.3 0.1 pad_add_fusion.2
  3.4 2.4 %collective-permute-start = (f32[3,8,128]{2,0,1:T(4,128)S(1)}, f32[3,8,128]{2,0,1:T(4,128)S(1)}, u32[]{:S(2)}, u32[]{:S(2)}) collective-permute-start(f32[3,8,128]{2,0,1:T(4,128)S(1)} %get-tuple-element.367), channel_id=1, source_target_pairs={{0,4},{4,8},{8,12},{1,5},{5,9},{9,13},{2,6},{6,10},{10,14},{3,7},{... | collective-permute-start | bytes 36872 | tf_op jit(solution)/shard_map/ppermute | solution.py:17
  5.8 1.3 collective-permute-start.1
  7.1 0.0 copy-start.4
  7.1 0.0 copy-start.5
  7.1 0.7 copy-done.4
  7.8 0.0 copy-done.5
  7.8 0.7 fusion.70
  19.3 13.4 %psum.28 = f32[2,3,8,128]{3,1,2,0:T(4,128)S(1)} all-reduce(f32[2,3,8,128]{3,1,2,0:T(4,128)S(1)} %pad_maximum_fusion), channel_id=1, replica_groups=mesh['face'=2,'ty'=4,'tx'=4] {'ty'}, use_global_device_ids=true, to_apply=%region_0.1 | all-reduce | flops 6144 | bytes 49152 | tf_op jit(solution)/shard_map/psum | solution.py:160
  32.7 13.6 %all_gather.24 = f32[2,3,32,128]{3,1,2,0:T(4,128)S(1)} all-gather(f32[2,3,8,128]{3,1,2,0:T(4,128)S(1)} %psum.28), channel_id=1, replica_groups=mesh['face'=2,'ty'=4,'tx'=4] {'tx'}, dimensions={2}, use_global_device_ids=true | all-gather | bytes 122880 | tf_op jit(solution)/shard_map/all_gather | solution.py:161
  46.3 5.3 %all-gather = f32[4,3,32,128]{3,2,1,0:T(8,128)S(1)} all-gather(f32[2,3,32,128]{3,2,1,0:T(8,128)S(1)} %copy.69), channel_id=2, replica_groups=mesh['face'=2,'ty'=4,'tx'=4] {'face'}, dimensions={0}, use_global_device_ids=true | all-gather | bytes 294912 | tf_op jit(solution)/shard_map/all_gather | solution.py:89
  51.6 0.7 fusion.69
  55.2 0.1 scatter-add.85
  55.4 0.0 copy-start.1
  55.4 0.7 copy-done.1
  56.2 0.0 copy-start.3
  56.2 0.1 tile.25
  56.3 0.1 scatter-add.89
  56.5 0.4 copy-done.3
  56.9 0.1 copy.72
  57.0 0.1 scatter-add.80
  57.1 0.1 scatter-add.81
  57.3 0.1 fusion.67
  57.4 0.1 fusion.29
  57.5 3.5 %collective-permute-start.2 = (f32[8,3,128]{2,0,1:T(8,128)S(1)}, f32[8,3,128]{2,0,1:T(8,128)S(1)}, u32[]{:S(2)}, u32[]{:S(2)}) collective-permute-start(f32[8,3,128]{2,0,1:T(8,128)S(1)} %get-tuple-element.333), channel_id=1, source_target_pairs={{0,1},{1,2},{2,3},{4,5},{5,6},{6,7},{8,9},{9,10},{10,11},{12,13},{... | collective-permute-start | bytes 36872 | tf_op jit(solution)/shard_map/ppermute | solution.py:17
  61.1 1.3 collective-permute-start.3
  62.4 20.3 %psum.29 = f32[2,3,8,128]{3,2,1,0:T(8,128)S(1)} all-reduce(f32[2,3,8,128]{3,2,1,0:T(8,128)S(1)} %pad_maximum_fusion.2), channel_id=1, replica_groups=mesh['face'=2,'ty'=4,'tx'=4] {'tx'}, use_global_device_ids=true, to_apply=%region_1.2 | all-reduce | flops 6144 | bytes 49152 | tf_op jit(solution)/shard_map/psum | solution.py:139
  82.6 5.3 %all_gather.26 = f32[2,3,32,128]{3,2,1,0:T(8,128)S(1)} all-gather(f32[2,3,8,128]{3,2,1,0:T(8,128)S(1)} %psum.29), channel_id=1, replica_groups=mesh['face'=2,'ty'=4,'tx'=4] {'ty'}, dimensions={2}, use_global_device_ids=true | all-gather | bytes 122880 | tf_op jit(solution)/shard_map/all_gather | solution.py:140
  88.0 5.7 %all-gather.1 = f32[4,3,32,128]{3,2,1,0:T(8,128)S(1)} all-gather(f32[2,3,32,128]{3,2,1,0:T(8,128)S(1)} %all_gather.26), channel_id=3, replica_groups=mesh['face'=2,'ty'=4,'tx'=4] {'face'}, dimensions={0}, use_global_device_ids=true | all-gather | bytes 294912 | tf_op jit(solution)/shard_map/all_gather | solution.py:89
  94.0 0.1 scatter-add.95
  94.2 0.1 scatter-add.99
  94.3 0.0 collective-permute-done.2
  94.4 0.1 fusion.66
  94.5 0.1 fusion.20
  94.6 0.1 pad_add_fusion
  94.7 1.3 collective-permute-start.5
  96.1 3.0 %collective-permute-start.4 = (f32[3,8,128]{2,0,1:T(4,128)S(1)}, f32[3,8,128]{2,0,1:T(4,128)S(1)}, u32[]{:S(2)}, u32[]{:S(2)}) collective-permute-start(f32[3,8,128]{2,0,1:T(4,128)S(1)} %get-tuple-element.364), channel_id=1, source_target_pairs={{0,4},{4,8},{8,12},{1,5},{5,9},{9,13},{2,6},{6,10},{10,14},{3,7},{... | collective-permute-start | bytes 36872 | tf_op jit(solution)/shard_map/ppermute | solution.py:17
  99.1 11.7 %psum.30 = f32[2,3,8,128]{3,1,2,0:T(4,128)S(1)} all-reduce(f32[2,3,8,128]{3,1,2,0:T(4,128)S(1)} %pad_maximum_fusion.1), channel_id=1, replica_groups=mesh['face'=2,'ty'=4,'tx'=4] {'ty'}, use_global_device_ids=true, to_apply=%region_2.3 | all-reduce | flops 6144 | bytes 49152 | tf_op jit(solution)/shard_map/psum | solution.py:160
  110.8 13.5 %all_gather.28 = f32[2,3,32,128]{3,1,2,0:T(4,128)S(1)} all-gather(f32[2,3,8,128]{3,1,2,0:T(4,128)S(1)} %psum.30), channel_id=1, replica_groups=mesh['face'=2,'ty'=4,'tx'=4] {'tx'}, dimensions={2}, use_global_device_ids=true | all-gather | bytes 122880 | tf_op jit(solution)/shard_map/all_gather | solution.py:161
  124.3 5.3 %all-gather.2 = f32[4,3,32,128]{3,2,1,0:T(8,128)S(1)} all-gather(f32[2,3,32,128]{3,2,1,0:T(8,128)S(1)} %copy.75), channel_id=4, replica_groups=mesh['face'=2,'ty'=4,'tx'=4] {'face'}, dimensions={0}, use_global_device_ids=true | all-gather | bytes 294912 | tf_op jit(solution)/shard_map/all_gather | solution.py:89
  129.9 0.1 scatter-add.105
  130.1 0.1 scatter-add.109
  130.3 0.1 scatter-add.100
  130.4 0.1 scatter-add.101
  130.6 0.1 fusion.65
  130.7 0.1 fusion.30
  130.9 1.3 collective-permute-start.7
  132.2 4.5 %collective-permute-start.6 = (f32[8,3,128]{2,0,1:T(8,128)S(1)}, f32[8,3,128]{2,0,1:T(8,128)S(1)}, u32[]{:S(2)}, u32[]{:S(2)}) collective-permute-start(f32[8,3,128]{2,0,1:T(8,128)S(1)} %get-tuple-element.321), channel_id=1, source_target_pairs={{0,1},{1,2},{2,3},{4,5},{5,6},{6,7},{8,9},{9,10},{10,11},{12,13},{... | collective-permute-start | bytes 36872 | tf_op jit(solution)/shard_map/ppermute | solution.py:17
  136.7 15.8 %psum.31 = f32[2,3,8,128]{3,2,1,0:T(8,128)S(1)} all-reduce(f32[2,3,8,128]{3,2,1,0:T(8,128)S(1)} %pad_maximum_fusion.3), channel_id=1, replica_groups=mesh['face'=2,'ty'=4,'tx'=4] {'tx'}, use_global_device_ids=true, to_apply=%region_3.4 | all-reduce | flops 6144 | bytes 49152 | tf_op jit(solution)/shard_map/psum | solution.py:139
  152.5 5.3 %all_gather.30 = f32[2,3,32,128]{3,2,1,0:T(8,128)S(1)} all-gather(f32[2,3,8,128]{3,2,1,0:T(8,128)S(1)} %psum.31), channel_id=1, replica_groups=mesh['face'=2,'ty'=4,'tx'=4] {'ty'}, dimensions={2}, use_global_device_ids=true | all-gather | bytes 122880 | tf_op jit(solution)/shard_map/all_gather | solution.py:140
  157.8 5.7 %all-gather.3 = f32[4,3,32,128]{3,2,1,0:T(8,128)S(1)} all-gather(f32[2,3,32,128]{3,2,1,0:T(8,128)S(1)} %all_gather.30), channel_id=5, replica_groups=mesh['face'=2,'ty'=4,'tx'=4] {'face'}, dimensions={0}, use_global_device_ids=true | all-gather | bytes 294912 | tf_op jit(solution)/shard_map/all_gather | solution.py:89
  163.8 0.1 scatter-add.115
  164.0 0.1 scatter-add.119
  164.2 0.0 collective-permute-done.7
  164.2 0.6 copy.80
  (106 shorter events, 1.5 us)
Async XLA Ops:
  1.6 0.8 copy-start
  2.4 0.7 copy-start.2
  3.4 53.6 %collective-permute-start = (f32[3,8,128]{2,0,1:T(4,128)S(1)}, f32[3,8,128]{2,0,1:T(4,128)S(1)}, u32[]{:S(2)}, u32[]{:S(2)}) collective-permute-start(f32[3,8,128]{2,0,1:T(4,128)S(1)} %get-tuple-element.367), channel_id=1, source_target_pairs={{0,4},{4,8},{8,12},{1,5},{5,9},{9,13},{2,6},{6,10},{10,14},{3,7},{... | collective-permute-start | bytes 36872 | tf_op jit(solution)/shard_map/ppermute | solution.py:17
  5.8 51.4 %collective-permute-start.1 = (f32[3,8,128]{2,0,1:T(4,128)S(1)}, f32[3,8,128]{2,0,1:T(4,128)S(1)}, u32[]{:S(2)}, u32[]{:S(2)}) collective-permute-start(f32[3,8,128]{2,0,1:T(4,128)S(1)} %get-tuple-element.366), channel_id=1, source_target_pairs={{4,0},{8,4},{12,8},{5,1},{9,5},{13,9},{6,2},{10,6},{14,10},{7,3},{... | collective-permute-start | bytes 36872 | tf_op jit(solution)/shard_map/ppermute | solution.py:19
  7.1 0.7 copy-start.4
  7.1 0.7 copy-start.5
  55.4 0.8 copy-start.1
  56.2 0.7 copy-start.3
  57.5 36.8 %collective-permute-start.2 = (f32[8,3,128]{2,0,1:T(8,128)S(1)}, f32[8,3,128]{2,0,1:T(8,128)S(1)}, u32[]{:S(2)}, u32[]{:S(2)}) collective-permute-start(f32[8,3,128]{2,0,1:T(8,128)S(1)} %get-tuple-element.333), channel_id=1, source_target_pairs={{0,1},{1,2},{2,3},{4,5},{5,6},{6,7},{8,9},{9,10},{10,11},{12,13},{... | collective-permute-start | bytes 36872 | tf_op jit(solution)/shard_map/ppermute | solution.py:17
  61.1 33.3 %collective-permute-start.3 = (f32[8,3,128]{2,0,1:T(8,128)S(1)}, f32[8,3,128]{2,0,1:T(8,128)S(1)}, u32[]{:S(2)}, u32[]{:S(2)}) collective-permute-start(f32[8,3,128]{2,0,1:T(8,128)S(1)} %get-tuple-element.307), channel_id=1, source_target_pairs={{1,0},{2,1},{3,2},{5,4},{6,5},{7,6},{9,8},{10,9},{11,10},{13,12},{... | collective-permute-start | bytes 36872 | tf_op jit(solution)/shard_map/ppermute | solution.py:19
  94.7 35.7 %collective-permute-start.5 = (f32[3,8,128]{2,0,1:T(4,128)S(1)}, f32[3,8,128]{2,0,1:T(4,128)S(1)}, u32[]{:S(2)}, u32[]{:S(2)}) collective-permute-start(f32[3,8,128]{2,0,1:T(4,128)S(1)} %get-tuple-element.363), channel_id=1, source_target_pairs={{4,0},{8,4},{12,8},{5,1},{9,5},{13,9},{6,2},{10,6},{14,10},{7,3},{... | collective-permute-start | bytes 36872 | tf_op jit(solution)/shard_map/ppermute | solution.py:19
  96.1 34.2 %collective-permute-start.4 = (f32[3,8,128]{2,0,1:T(4,128)S(1)}, f32[3,8,128]{2,0,1:T(4,128)S(1)}, u32[]{:S(2)}, u32[]{:S(2)}) collective-permute-start(f32[3,8,128]{2,0,1:T(4,128)S(1)} %get-tuple-element.364), channel_id=1, source_target_pairs={{0,4},{4,8},{8,12},{1,5},{5,9},{9,13},{2,6},{6,10},{10,14},{3,7},{... | collective-permute-start | bytes 36872 | tf_op jit(solution)/shard_map/ppermute | solution.py:17
  130.9 33.4 %collective-permute-start.7 = (f32[8,3,128]{2,0,1:T(8,128)S(1)}, f32[8,3,128]{2,0,1:T(8,128)S(1)}, u32[]{:S(2)}, u32[]{:S(2)}) collective-permute-start(f32[8,3,128]{2,0,1:T(8,128)S(1)} %get-tuple-element.295), channel_id=1, source_target_pairs={{1,0},{2,1},{3,2},{5,4},{6,5},{7,6},{9,8},{10,9},{11,10},{13,12},{... | collective-permute-start | bytes 36872 | tf_op jit(solution)/shard_map/ppermute | solution.py:19
  132.2 32.0 %collective-permute-start.6 = (f32[8,3,128]{2,0,1:T(8,128)S(1)}, f32[8,3,128]{2,0,1:T(8,128)S(1)}, u32[]{:S(2)}, u32[]{:S(2)}) collective-permute-start(f32[8,3,128]{2,0,1:T(8,128)S(1)} %get-tuple-element.321), channel_id=1, source_target_pairs={{0,1},{1,2},{2,3},{4,5},{5,6},{6,7},{8,9},{9,10},{10,11},{12,13},{... | collective-permute-start | bytes 36872 | tf_op jit(solution)/shard_map/ppermute | solution.py:17
where the time goes:
time: 166 us; the launch traced here: 165 us
  blocking collectives  121 us (73%)
  starting transfers between devices  18.7 us (11%)
  between operations  14.5 us (9%)
  local copies, waits for them, and re-layouts  9.41 us (6%)
    psum x2, blocking collectives, reverse_x(): row_total = lax.psum(pieces, 'tx')  36 us
    all_gather x2, blocking collectives, reverse_y(): strips = lax.all_gather(column_total, 'tx', axis=2, tiled=True)  27.1 us
    psum x2, blocking collectives, reverse_y(): column_total = lax.psum(pieces, 'ty')  25.1 us
    all_gather x4, blocking collectives, deliver(): gathered = lax.all_gather(strips[None], 'face', axis=0, tiled=True)  22 us
    ppermute x4, starting transfers between devices, padded(): lax.ppermute(tail, axis, [(i, (i + 1) % count) for i in range(ends)])  13.5 us
    all_gather x2, blocking collectives, reverse_x(): strips = lax.all_gather(row_total, 'ty', axis=2, tiled=True)  10.6 us
    ppermute x4, starting transfers between devices, padded(): lax.ppermute(head, axis, [((i + 1) % count, i) for i in range(ends)])  5.17 us
  transfers between devices with their start and end apart: 8, of which 0 were waited for; matrix products, arithmetic and copies ran while one was open for 3% of the time, Pallas kernels for 0%

commit v1 on v0

--- a/solution.py
+++ b/solution.py
@@ -2,6 +2,7 @@
 import jax.numpy as jnp
 from jax import lax
 from jax.sharding import PartitionSpec as P
+from jax.lax import axis_index, ppermute, psum
 
 STEPS = 2
 
@@ -86,7 +87,19 @@
     on_south = indicator(row_index == 0)
 
     def deliver(strips, parity):
-        gathered = lax.all_gather(strips[None], "face", axis=0, tiled=True)
+
+        def find_weights_on(shard_in):
+            back, arr_next = (psum(1, "face"), axis_index("face"))
+            heard, later = (shard_in, 1)
+            while later < back:
+                z2 = ppermute(heard, "face", tuple(((pp, pp ^ later) for pp in range(back))))
+                lower = jnp.concatenate([heard, z2], 0)
+                last = jnp.concatenate([z2, heard], 0)
+                heard = jnp.where(arr_next & later == 0, lower, last)
+                later = 2 * later
+            return heard
+
+        gathered = find_weights_on(strips[None])
         result = jnp.zeros((height_cells, width_cells, lanes_all), jnp.float32)
         for border in range(4):
             code = own_codes[border]

time: 166 us -> 160 us (0.964)
  blocking collectives: 121 us -> 100 us
  waiting for transfers between devices: 0.02 us -> 12.8 us
    all_gather x4 -> x0, blocking collectives: 22 us -> none  [deliver(): gathered = lax.all_gather(strips[None], 'face', axis=0, tiled=True)]
    ppermute x0 -> x4, waiting for transfers between devices: none -> 12.8 us  [find_weights_on(): ppermute(heard, 'face', tuple(((pp, pp ^ later) for pp in range(back))))]
    ppermute x0 -> x4, starting transfers between devices: none -> 3.04 us  [find_weights_on(): ppermute(heard, 'face', tuple(((pp, pp ^ later) for pp in range(back))))]
    unnamed x13 -> x16, local copies, waits for them, and re-layouts: 3.12 us -> 3.32 us
  transfers between devices with their start and end apart: 8 -> 12, of which waited for: 0 -> 3; matrix products, arithmetic and copies ran while one was open for 3% -> 1% of each run, Pallas kernels for 0% -> 0%
where the time goes in v1:
time: 160 us; the launch traced here: 159 us
  blocking collectives  100 us (62%)
  starting transfers between devices  20.1 us (13%)
  between operations  14 us (9%)
  waiting for transfers between devices  12.8 us (8%)
  local copies, waits for them, and re-layouts  10.3 us (6%)
  other arithmetic  1.87 us (1%)
    psum x2, blocking collectives, reverse_x(): row_total = lax.psum(pieces, 'tx')  35.9 us
    all_gather x2, blocking collectives, reverse_y(): strips = lax.all_gather(column_total, 'tx', axis=2, tiled=True)  26.8 us
    psum x2, blocking collectives, reverse_y(): column_total = lax.psum(pieces, 'ty')  26.6 us
    ppermute x4, waiting for transfers between devices, find_weights_on(): ppermute(heard, 'face', tuple(((pp, pp ^ later) for pp in range(back))))  12.8 us
    ppermute x4, starting transfers between devices, padded(): lax.ppermute(tail, axis, [(i, (i + 1) % count) for i in range(ends)])  11.8 us
    all_gather x2, blocking collectives, reverse_x(): strips = lax.all_gather(row_total, 'ty', axis=2, tiled=True)  10.6 us
    ppermute x4, starting transfers between devices, padded(): lax.ppermute(head, axis, [((i + 1) % count, i) for i in range(ends)])  5.17 us
    unnamed x16, local copies, waits for them, and re-layouts  3.32 us
  transfers between devices with their start and end apart: 12, of which 3 were waited for; matrix products, arithmetic and copies ran while one was open for 1% of the time, Pallas kernels for 0%

profile of v1, /device:TPU:0, one launch (start us, length us, event | category | flops | bytes accessed | tf_op | source)
XLA Modules:
  0.0 159.1 jit_solution(17658043429511233421)
XLA Ops:
  0.0 0.8 copy.92
  0.8 0.8 tile.21
  1.6 0.0 copy-start.1
  1.6 0.1 tile.22
  1.7 0.6 copy-done.1
  2.3 0.1 fusion.64
  2.5 0.0 copy-start.2
  2.5 0.7 copy-done.2
  3.2 0.1 fusion.15
  3.3 0.1 pad_add_fusion.2
  3.4 2.4 %collective-permute-start = (f32[3,8,128]{2,0,1:T(4,128)S(1)}, f32[3,8,128]{2,0,1:T(4,128)S(1)}, u32[]{:S(2)}, u32[]{:S(2)}) collective-permute-start(f32[3,8,128]{2,0,1:T(4,128)S(1)} %get-tuple-element.367), channel_id=1, source_target_pairs={{0,4},{4,8},{8,12},{1,5},{5,9},{9,13},{2,6},{6,10},{10,14},{3,7},{... | collective-permute-start | bytes 36872 | tf_op jit(solution)/shard_map/ppermute | solution.py:18
  5.8 1.3 collective-permute-start.1
  7.2 13.4 %psum.28 = f32[2,3,8,128]{3,1,2,0:T(4,128)S(1)} all-reduce(f32[2,3,8,128]{3,1,2,0:T(4,128)S(1)} %pad_maximum_fusion), channel_id=1, replica_groups=mesh['face'=2,'ty'=4,'tx'=4] {'ty'}, use_global_device_ids=true, to_apply=%region_0.1 | all-reduce | flops 6144 | bytes 49152 | tf_op jit(solution)/shard_map/psum | solution.py:173
  20.6 13.6 %all_gather.12 = f32[2,3,32,128]{3,1,2,0:T(4,128)S(1)} all-gather(f32[2,3,8,128]{3,1,2,0:T(4,128)S(1)} %psum.28), channel_id=1, replica_groups=mesh['face'=2,'ty'=4,'tx'=4] {'tx'}, dimensions={2}, use_global_device_ids=true | all-gather | bytes 122880 | tf_op jit(solution)/shard_map/all_gather | solution.py:174
  34.2 1.5 collective-permute-start.2
  35.7 0.7 copy-done.5
  36.4 0.0 copy-done.6
  36.4 0.6 fusion.67
  38.3 0.7 fusion.66
  48.0 0.7 copy-done.3
  48.8 0.1 tile.25
  51.5 0.1 copy.100
  51.6 0.1 scatter-add.80
  51.8 0.1 scatter-add.81
  52.0 0.1 maximum_select_fusion
  52.0 0.1 dynamic-slice_bitcast_fusion
  52.3 0.1 scatter-add.85
  52.5 0.1 scatter-add.89
  52.7 0.1 fusion.63
  52.7 0.1 fusion.25
  52.9 3.5 %collective-permute-start.3 = (f32[8,3,128]{2,0,1:T(8,128)S(1)}, f32[8,3,128]{2,0,1:T(8,128)S(1)}, u32[]{:S(2)}, u32[]{:S(2)}) collective-permute-start(f32[8,3,128]{2,0,1:T(8,128)S(1)} %get-tuple-element.339), channel_id=1, source_target_pairs={{0,1},{1,2},{2,3},{4,5},{5,6},{6,7},{8,9},{9,10},{10,11},{12,13},{... | collective-permute-start | bytes 36872 | tf_op jit(solution)/shard_map/ppermute | solution.py:18
  56.5 1.3 collective-permute-start.4
  57.8 20.2 %psum.29 = f32[2,3,8,128]{3,2,1,0:T(8,128)S(1)} all-reduce(f32[2,3,8,128]{3,2,1,0:T(8,128)S(1)} %pad_maximum_fusion.1), channel_id=1, replica_groups=mesh['face'=2,'ty'=4,'tx'=4] {'tx'}, use_global_device_ids=true, to_apply=%region_1.2 | all-reduce | flops 6144 | bytes 49152 | tf_op jit(solution)/shard_map/psum | solution.py:152
  78.0 5.3 %all_gather.13 = f32[2,3,32,128]{3,2,1,0:T(8,128)S(1)} all-gather(f32[2,3,8,128]{3,2,1,0:T(8,128)S(1)} %psum.29), channel_id=1, replica_groups=mesh['face'=2,'ty'=4,'tx'=4] {'ty'}, dimensions={2}, use_global_device_ids=true | all-gather | bytes 122880 | tf_op jit(solution)/shard_map/all_gather | solution.py:153
  83.3 0.5 collective-permute-start.5
  83.8 4.5 %collective-permute-done.5 = f32[1,2,3,32,128]{4,3,2,1,0:T(8,128)S(1)} collective-permute-done((f32[1,2,3,32,128]{4,3,2,1,0:T(8,128)S(1)}, f32[1,2,3,32,128]{4,3,2,1,0:T(8,128)S(1)}, u32[]{:S(2)}, u32[]{:S(2)}) %collective-permute-start.5) | collective-permute-done | bytes 98336 | tf_op jit(solution)/shard_map/ppermute | solution.py:95
  88.7 0.1 scatter-add.95
  88.8 0.1 scatter-add.99
  89.0 0.1 fusion.62
  89.1 0.1 fusion.18
  89.3 0.1 copy_add_fusion
  89.6 0.6 copy-done
  90.2 0.7 slice-done
  91.0 1.4 collective-permute-start.6
  92.4 1.3 collective-permute-start.7
  93.7 13.2 %psum.30 = f32[2,3,8,128]{3,2,1,0:T(8,128)S(1)} all-reduce(f32[2,3,8,128]{3,2,1,0:T(8,128)S(1)} %pad_maximum_fusion.2), channel_id=1, replica_groups=mesh['face'=2,'ty'=4,'tx'=4] {'ty'}, use_global_device_ids=true, to_apply=%region_2.3 | all-reduce | flops 6144 | bytes 49152 | tf_op jit(solution)/shard_map/psum | solution.py:173
  106.9 13.2 %all_gather.14 = f32[2,3,32,128]{3,2,1,0:T(8,128)S(1)} all-gather(f32[2,3,8,128]{3,2,1,0:T(8,128)S(1)} %psum.30), channel_id=1, replica_groups=mesh['face'=2,'ty'=4,'tx'=4] {'tx'}, dimensions={2}, use_global_device_ids=true | all-gather | bytes 122880 | tf_op jit(solution)/shard_map/all_gather | solution.py:174
  120.2 0.5 collective-permute-start.8
  120.7 0.1 scatter-add.100
  120.9 0.1 scatter-add.101
  121.0 3.8 %collective-permute-done.8 = f32[1,2,3,32,128]{4,3,2,1,0:T(8,128)S(1)} collective-permute-done((f32[1,2,3,32,128]{4,3,2,1,0:T(8,128)S(1)}, f32[1,2,3,32,128]{4,3,2,1,0:T(8,128)S(1)}, u32[]{:S(2)}, u32[]{:S(2)}) %collective-permute-start.8) | collective-permute-done | bytes 98336 | tf_op jit(solution)/shard_map/ppermute | solution.py:95
  125.1 0.1 scatter-add.105
  125.3 0.1 scatter-add.109
  125.5 0.1 fusion.61
  125.5 0.1 fusion.26
  125.7 1.3 collective-permute-start.10
  127.1 4.5 %collective-permute-start.9 = (f32[8,3,128]{2,0,1:T(8,128)S(1)}, f32[8,3,128]{2,0,1:T(8,128)S(1)}, u32[]{:S(2)}, u32[]{:S(2)}) collective-permute-start(f32[8,3,128]{2,0,1:T(8,128)S(1)} %get-tuple-element.329), channel_id=1, source_target_pairs={{0,1},{1,2},{2,3},{4,5},{5,6},{6,7},{8,9},{9,10},{10,11},{12,13},{... | collective-permute-start | bytes 36872 | tf_op jit(solution)/shard_map/ppermute | solution.py:18
  131.6 15.8 %psum.31 = f32[2,3,8,128]{3,2,1,0:T(8,128)S(1)} all-reduce(f32[2,3,8,128]{3,2,1,0:T(8,128)S(1)} %pad_maximum_fusion.3), channel_id=1, replica_groups=mesh['face'=2,'ty'=4,'tx'=4] {'tx'}, use_global_device_ids=true, to_apply=%region_3.4 | all-reduce | flops 6144 | bytes 49152 | tf_op jit(solution)/shard_map/psum | solution.py:152
  147.4 5.3 %all_gather.15 = f32[2,3,32,128]{3,2,1,0:T(8,128)S(1)} all-gather(f32[2,3,8,128]{3,2,1,0:T(8,128)S(1)} %psum.31), channel_id=1, replica_groups=mesh['face'=2,'ty'=4,'tx'=4] {'ty'}, dimensions={2}, use_global_device_ids=true | all-gather | bytes 122880 | tf_op jit(solution)/shard_map/all_gather | solution.py:153
  152.7 0.5 collective-permute-start.11
  153.3 4.5 %collective-permute-done.11 = f32[1,2,3,32,128]{4,3,2,1,0:T(8,128)S(1)} collective-permute-done((f32[1,2,3,32,128]{4,3,2,1,0:T(8,128)S(1)}, f32[1,2,3,32,128]{4,3,2,1,0:T(8,128)S(1)}, u32[]{:S(2)}, u32[]{:S(2)}) %collective-permute-start.11) | collective-permute-done | bytes 98336 | tf_op jit(solution)/shard_map/ppermute | solution.py:95
  158.1 0.1 scatter-add.115
  158.3 0.1 scatter-add.119
  158.4 0.6 copy.129
  (128 shorter events, 1.7 us)
Async XLA Ops:
  1.6 0.8 copy-start.1
  2.5 0.7 copy-start.2
  3.4 48.2 %collective-permute-start = (f32[3,8,128]{2,0,1:T(4,128)S(1)}, f32[3,8,128]{2,0,1:T(4,128)S(1)}, u32[]{:S(2)}, u32[]{:S(2)}) collective-permute-start(f32[3,8,128]{2,0,1:T(4,128)S(1)} %get-tuple-element.367), channel_id=1, source_target_pairs={{0,4},{4,8},{8,12},{1,5},{5,9},{9,13},{2,6},{6,10},{10,14},{3,7},{... | collective-permute-start | bytes 36872 | tf_op jit(solution)/shard_map/ppermute | solution.py:18
  5.8 46.0 %collective-permute-start.1 = (f32[3,8,128]{2,0,1:T(4,128)S(1)}, f32[3,8,128]{2,0,1:T(4,128)S(1)}, u32[]{:S(2)}, u32[]{:S(2)}) collective-permute-start(f32[3,8,128]{2,0,1:T(4,128)S(1)} %get-tuple-element.366), channel_id=1, source_target_pairs={{4,0},{8,4},{12,8},{5,1},{9,5},{13,9},{6,2},{10,6},{14,10},{7,3},{... | collective-permute-start | bytes 36872 | tf_op jit(solution)/shard_map/ppermute | solution.py:20
  34.2 17.8 %collective-permute-start.2 = (f32[1,2,3,32,128]{4,2,3,1,0:T(4,128)S(1)}, f32[1,2,3,32,128]{4,2,3,1,0:T(4,128)S(1)}, u32[]{:S(2)}, u32[]{:S(2)}) collective-permute-start(f32[1,2,3,32,128]{4,2,3,1,0:T(4,128)S(1)} %bitcast.117), channel_id=1, source_target_pairs={{0,16},{16,0},{1,17},{17,1},{2,18},{18,2},{3,19},{19,3},{4,20},{20... | collective-permute-start | bytes 294920 | tf_op jit(solution)/shard_map/ppermute | solution.py:95
  35.7 0.7 copy-start.5
  35.7 0.7 copy-start.6
  48.0 0.8 copy-start.3
  50.8 0.7 copy-start.4
  52.9 30.8 %collective-permute-start.3 = (f32[8,3,128]{2,0,1:T(8,128)S(1)}, f32[8,3,128]{2,0,1:T(8,128)S(1)}, u32[]{:S(2)}, u32[]{:S(2)}) collective-permute-start(f32[8,3,128]{2,0,1:T(8,128)S(1)} %get-tuple-element.339), channel_id=1, source_target_pairs={{0,1},{1,2},{2,3},{4,5},{5,6},{6,7},{8,9},{9,10},{10,11},{12,13},{... | collective-permute-start | bytes 36872 | tf_op jit(solution)/shard_map/ppermute | solution.py:18
  56.5 27.3 %collective-permute-start.4 = (f32[8,3,128]{2,0,1:T(8,128)S(1)}, f32[8,3,128]{2,0,1:T(8,128)S(1)}, u32[]{:S(2)}, u32[]{:S(2)}) collective-permute-start(f32[8,3,128]{2,0,1:T(8,128)S(1)} %get-tuple-element.311), channel_id=1, source_target_pairs={{1,0},{2,1},{3,2},{5,4},{6,5},{7,6},{9,8},{10,9},{11,10},{13,12},{... | collective-permute-start | bytes 36872 | tf_op jit(solution)/shard_map/ppermute | solution.py:20
  83.3 5.0 %collective-permute-start.5 = (f32[1,2,3,32,128]{4,3,2,1,0:T(8,128)S(1)}, f32[1,2,3,32,128]{4,3,2,1,0:T(8,128)S(1)}, u32[]{:S(2)}, u32[]{:S(2)}) collective-permute-start(f32[1,2,3,32,128]{4,3,2,1,0:T(8,128)S(1)} %bitcast.121), channel_id=1, source_target_pairs={{0,16},{16,0},{1,17},{17,1},{2,18},{18,2},{3,19},{19,3},{4,20},{20... | collective-permute-start | bytes 294920 | tf_op jit(solution)/shard_map/ppermute | solution.py:95
  89.6 0.6 copy-start
  90.2 0.8 slice-start
  91.0 29.7 %collective-permute-start.6 = (f32[3,8,128]{2,0,1:T(4,128)S(1)}, f32[3,8,128]{2,0,1:T(4,128)S(1)}, u32[]{:S(2)}, u32[]{:S(2)}) collective-permute-start(f32[3,8,128]{2,0,1:T(4,128)S(1)} %get-tuple-element.372), channel_id=1, source_target_pairs={{0,4},{4,8},{8,12},{1,5},{5,9},{9,13},{2,6},{6,10},{10,14},{3,7},{... | collective-permute-start | bytes 36872 | tf_op jit(solution)/shard_map/ppermute | solution.py:18
  92.4 28.5 %collective-permute-start.7 = (f32[3,8,128]{2,0,1:T(4,128)S(1)}, f32[3,8,128]{2,0,1:T(4,128)S(1)}, u32[]{:S(2)}, u32[]{:S(2)}) collective-permute-start(f32[3,8,128]{2,0,1:T(4,128)S(1)} %copy.118), channel_id=1, source_target_pairs={{4,0},{8,4},{12,8},{5,1},{9,5},{13,9},{6,2},{10,6},{14,10},{7,3},{... | collective-permute-start | bytes 36872 | tf_op jit(solution)/shard_map/ppermute | solution.py:20
  120.2 4.6 %collective-permute-start.8 = (f32[1,2,3,32,128]{4,3,2,1,0:T(8,128)S(1)}, f32[1,2,3,32,128]{4,3,2,1,0:T(8,128)S(1)}, u32[]{:S(2)}, u32[]{:S(2)}) collective-permute-start(f32[1,2,3,32,128]{4,3,2,1,0:T(8,128)S(1)} %bitcast.123), channel_id=1, source_target_pairs={{0,16},{16,0},{1,17},{17,1},{2,18},{18,2},{3,19},{19,3},{4,20},{20... | collective-permute-start | bytes 294920 | tf_op jit(solution)/shard_map/ppermute | solution.py:95
  125.7 27.5 %collective-permute-start.10 = (f32[8,3,128]{2,0,1:T(8,128)S(1)}, f32[8,3,128]{2,0,1:T(8,128)S(1)}, u32[]{:S(2)}, u32[]{:S(2)}) collective-permute-start(f32[8,3,128]{2,0,1:T(8,128)S(1)} %get-tuple-element.295), channel_id=1, source_target_pairs={{1,0},{2,1},{3,2},{5,4},{6,5},{7,6},{9,8},{10,9},{11,10},{13,12},{... | collective-permute-start | bytes 36872 | tf_op jit(solution)/shard_map/ppermute | solution.py:20
  127.1 26.2 %collective-permute-start.9 = (f32[8,3,128]{2,0,1:T(8,128)S(1)}, f32[8,3,128]{2,0,1:T(8,128)S(1)}, u32[]{:S(2)}, u32[]{:S(2)}) collective-permute-start(f32[8,3,128]{2,0,1:T(8,128)S(1)} %get-tuple-element.329), channel_id=1, source_target_pairs={{0,1},{1,2},{2,3},{4,5},{5,6},{6,7},{8,9},{9,10},{10,11},{12,13},{... | collective-permute-start | bytes 36872 | tf_op jit(solution)/shard_map/ppermute | solution.py:18
  152.7 5.0 %collective-permute-start.11 = (f32[1,2,3,32,128]{4,3,2,1,0:T(8,128)S(1)}, f32[1,2,3,32,128]{4,3,2,1,0:T(8,128)S(1)}, u32[]{:S(2)}, u32[]{:S(2)}) collective-permute-start(f32[1,2,3,32,128]{4,3,2,1,0:T(8,128)S(1)} %bitcast.119), channel_id=1, source_target_pairs={{0,16},{16,0},{1,17},{17,1},{2,18},{18,2},{3,19},{19,3},{4,20},{20... | collective-permute-start | bytes 294920 | tf_op jit(solution)/shard_map/ppermute | solution.py:95
